TPU v7x, 32 devices: a whole 2x2x4 slice. The times are simulated.
32 devices in a mesh: rep: 4 (over z), fsdp: 2 (over x), seq: 4 (over y, core).
Axes of the slice: x: 2, y: 2, z: 4, core: 2. Of those that a mesh axis runs over, the one named last changes fastest.
Arguments:
- tokens: bfloat16 [8, 1024, 640], P(('rep', 'fsdp'), 'seq'), may hold values from -6 to 6
- d_out: bfloat16 [8, 1024, 640], P(('rep', 'fsdp'), 'seq'), may hold values from -6 to 6
- doc_lengths: int32 [8, 3], P(('rep', 'fsdp')), may hold values from 1 to 640, 1024 in all within a row
- w_query: bfloat16 [640, 1024], P('fsdp'), may hold values from -0.25 to 0.25
- w_key: bfloat16 [640, 256], P('fsdp'), may hold values from -0.25 to 0.25
- w_value: bfloat16 [640, 256], P('fsdp'), may hold values from -0.25 to 0.25
- w_out: bfloat16 [1024, 640], P('fsdp'), may hold values from -0.1875 to 0.1875
- w_gate: bfloat16 [640, 2048], P('fsdp'), may hold values from -0.25 to 0.25
- w_up: bfloat16 [640, 2048], P('fsdp'), may hold values from -0.25 to 0.25
- w_down: bfloat16 [2048, 640], P('fsdp'), may hold values from -0.125 to 0.125
- g_input: bfloat16 [640], P('fsdp'), may hold values from 0.5 to 1.5
- g_query: bfloat16 [256], P('fsdp'), may hold values from 0.25 to 1.75
- g_key: bfloat16 [256], P('fsdp'), may hold values from 0.25 to 1.75
- g_attn: bfloat16 [640], P('fsdp'), may hold values from 0.5 to 1.5
- g_ffin: bfloat16 [640], P('fsdp'), may hold values from 0.5 to 1.5
- g_ffout: bfloat16 [640], P('fsdp'), may hold values from 0.5 to 1.5
Outputs:
- result: bfloat16 [8, 1024, 640], P(('rep', 'fsdp'), 'seq')
- d_tokens: bfloat16 [8, 1024, 640], P(('rep', 'fsdp'), 'seq')
- grad_query: float32 [640, 1024], P('fsdp')
- grad_key: float32 [640, 256], P('fsdp')
- grad_value: float32 [640, 256], P('fsdp')
- grad_out: float32 [1024, 640], P('fsdp')
- grad_gate: float32 [640, 2048], P('fsdp')
- grad_up: float32 [640, 2048], P('fsdp')
- grad_down: float32 [2048, 640], P('fsdp')
- grad_ginput: float32 [640], P('fsdp')
- grad_gquery: float32 [256], P('fsdp')
- grad_gkey: float32 [256], P('fsdp')
- grad_gattn: float32 [640], P('fsdp')
- grad_gffin: float32 [640], P('fsdp')
- grad_gffout: float32 [640], P('fsdp')
Inputs may be any that keep to these rules, and one draw needn't show every extreme that they name: `doc_lengths`: each row lists the lengths of the 3 documents packed in order into one sequence; a row sums to 1024 and its largest entry is 640.
All inputs are finite; a program needn't handle non-finite values.
Results may differ from a plain program's by a relative error of at most 0.024.
Values may be sent and summed in bfloat16 or wider, within the bound.
A program may use at most 128 MiB of HBM per device.

v0:
```python
import jax
import jax.numpy as jnp
from jax import lax
from jax.sharding import PartitionSpec as P

EPS = 1e-06
ROPE_BASE = 1000000.0
MASKED = -1e30


def rms_norm(values, gain_vec):
    return values * lax.rsqrt(jnp.mean(values * values, axis=-1, keepdims=True) + EPS) * gain_vec


def rotate(values, angles):
    half_width = values.shape[-1] // 2
    front_half = values[..., :half_width]
    back_half = values[..., half_width:]
    cos_part = jnp.cos(angles)
    sin_part = jnp.sin(angles)
    return jnp.concatenate(
        [
            front_half * cos_part - back_half * sin_part,
            back_half * cos_part + front_half * sin_part,
        ],
        axis=-1,
    )


def frequencies(head_size):
    return jnp.power(
        jnp.float32(ROPE_BASE), -2.0 * jnp.arange(head_size // 2, dtype=jnp.float32) / head_size
    )


def layout(lengths_row, total_len):
    doc_ends = jnp.cumsum(lengths_row)
    starts = doc_ends - lengths_row
    indices = jnp.arange(total_len, dtype=jnp.int32)
    segment = jnp.sum((indices[:, None] >= doc_ends[None, :]).astype(jnp.int32), axis=1)
    onehot = segment[:, None] == jnp.arange(lengths_row.shape[0], dtype=jnp.int32)[None, :]
    doc_begin = jnp.sum(jnp.where(onehot, starts[None, :], 0), axis=1)
    return (segment, indices - doc_begin)


def matmul(left_side, right_side):
    return jnp.dot(left_side, right_side, preferred_element_type=jnp.float32)


def times_transpose(left_side, right_side):
    return lax.dot_general(
        left_side, right_side, (((1,), (1,)), ((), ())), preferred_element_type=jnp.float32
    )


def transpose_times(left_side, right_side):
    return lax.dot_general(
        left_side, right_side, (((0,), (0,)), ((), ())), preferred_element_type=jnp.float32
    )


def gated(gate_proj, up_proj):
    return jax.nn.gelu(gate_proj, approximate=True) * up_proj


def body(
    tokens,
    d_out,
    doc_lengths,
    w_query,
    w_key,
    w_value,
    w_out,
    w_gate,
    w_up,
    w_down,
    g_input,
    g_query,
    g_key,
    g_attn,
    g_ffin,
    g_ffout,
):
    gathered = (
        lax.all_gather(w_query, "fsdp", axis=0, tiled=True),
        lax.all_gather(w_key, "fsdp", axis=0, tiled=True),
        lax.all_gather(w_value, "fsdp", axis=0, tiled=True),
        lax.all_gather(w_out, "fsdp", axis=0, tiled=True),
        lax.all_gather(w_gate, "fsdp", axis=0, tiled=True),
        lax.all_gather(w_up, "fsdp", axis=0, tiled=True),
        lax.all_gather(w_down, "fsdp", axis=0, tiled=True),
        lax.all_gather(g_input, "fsdp", axis=0, tiled=True),
        lax.all_gather(g_query, "fsdp", axis=0, tiled=True),
        lax.all_gather(g_key, "fsdp", axis=0, tiled=True),
        lax.all_gather(g_attn, "fsdp", axis=0, tiled=True),
        lax.all_gather(g_ffin, "fsdp", axis=0, tiled=True),
        lax.all_gather(g_ffout, "fsdp", axis=0, tiled=True),
    )
    query_mat, key_mat, value_mat, out_mat, gate_mat, up_mat, down_mat = gathered[:7]
    gain_input, gain_query, gain_key, gain_attn, gain_ffin, gain_ffout = [
        entry.astype(jnp.float32) for entry in gathered[7:]
    ]
    row_count = tokens.shape[1]
    head_size = gain_query.shape[0]
    head_count = query_mat.shape[1] // head_size
    total_len = row_count * lax.axis_size("seq")
    segment, position = layout(doc_lengths[0], total_len)
    offset = lax.axis_index("seq") * row_count
    query_seg = lax.dynamic_slice_in_dim(segment, offset, row_count)
    query_pos = lax.dynamic_slice_in_dim(position, offset, row_count)
    places = offset + jnp.arange(row_count, dtype=jnp.int32)
    allowed = (query_seg[:, None] == segment[None, :]) & (
        places[:, None] >= jnp.arange(total_len, dtype=jnp.int32)[None, :]
    )
    angles = query_pos.astype(jnp.float32)[:, None] * frequencies(head_size)[None, :]
    scaling = head_size ** (-0.5)
    inputs = tokens[0].astype(jnp.float32)
    cotangent = d_out[0].astype(jnp.float32)
    input_norm, input_pull = jax.vjp(rms_norm, inputs, gain_input)
    attn_input = input_norm.astype(jnp.bfloat16)
    q_proj = matmul(attn_input, query_mat)
    k_proj = matmul(attn_input, key_mat)
    v_proj = matmul(attn_input, value_mat)

    def query_fn(projected, gain_vec):
        shaped = projected.reshape(projected.shape[0], -1, gain_vec.shape[0])
        return rotate(rms_norm(shaped, gain_vec), angles[:, None, :])

    def key_fn(projected, gain_vec):
        return rotate(rms_norm(projected, gain_vec), angles)

    queries, query_pull = jax.vjp(query_fn, q_proj, gain_query)
    keys_own, key_pull = jax.vjp(key_fn, k_proj, gain_key)
    query_rows = queries.astype(jnp.bfloat16).reshape(row_count * head_count, head_size)
    key_rows, value_rows = (
        lax.all_gather(keys_own.astype(jnp.bfloat16), "seq", axis=0, tiled=True),
        lax.all_gather(v_proj.astype(jnp.bfloat16), "seq", axis=0, tiled=True),
    )

    def masked_scores():
        raw_scores = times_transpose(query_rows, key_rows).reshape(row_count, head_count, total_len)
        return jnp.where(allowed[:, None, :], raw_scores * scaling, MASKED)

    scores = masked_scores()
    top_score = jnp.max(scores, axis=-1, keepdims=True)
    shifted = jnp.exp(scores - top_score)
    denominator = jnp.sum(shifted, axis=-1, keepdims=True)
    log_total = top_score + jnp.log(denominator)
    probs_low = (
        (shifted / denominator).astype(jnp.bfloat16).reshape(row_count * head_count, total_len)
    )
    mixed_rows = (
        matmul(probs_low, value_rows)
        .reshape(row_count, head_count * head_size)
        .astype(jnp.bfloat16)
    )
    out_proj = matmul(mixed_rows, out_mat)
    attn_norm, attn_pull = jax.vjp(rms_norm, out_proj, gain_attn)
    hidden_one = inputs + attn_norm
    ffin_norm, ffin_pull = jax.vjp(rms_norm, hidden_one, gain_ffin)
    ff_input = ffin_norm.astype(jnp.bfloat16)
    gate_proj = matmul(ff_input, gate_mat)
    up_proj = matmul(ff_input, up_mat)
    activated, gated_pull = jax.vjp(gated, gate_proj, up_proj)
    hidden = activated.astype(jnp.bfloat16)
    down_proj = matmul(hidden, down_mat)
    ffout_norm, ffout_pull = jax.vjp(rms_norm, down_proj, gain_ffout)
    result = hidden_one + ffout_norm
    query_mat, key_mat, value_mat, out_mat, gate_mat, up_mat, down_mat = (
        lax.all_gather(w_query, "fsdp", axis=0, tiled=True),
        lax.all_gather(w_key, "fsdp", axis=0, tiled=True),
        lax.all_gather(w_value, "fsdp", axis=0, tiled=True),
        lax.all_gather(w_out, "fsdp", axis=0, tiled=True),
        lax.all_gather(w_gate, "fsdp", axis=0, tiled=True),
        lax.all_gather(w_up, "fsdp", axis=0, tiled=True),
        lax.all_gather(w_down, "fsdp", axis=0, tiled=True),
    )
    d_down, grad_gffout = ffout_pull(cotangent)
    d_down_low = d_down.astype(jnp.bfloat16)
    grad_down = transpose_times(hidden, d_down_low)
    d_hidden = times_transpose(d_down_low, down_mat)
    d_gate, d_up = gated_pull(d_hidden)
    d_gate_low = d_gate.astype(jnp.bfloat16)
    d_up_low = d_up.astype(jnp.bfloat16)
    grad_gate = transpose_times(ff_input, d_gate_low)
    grad_up = transpose_times(ff_input, d_up_low)
    d_ffin = times_transpose(d_gate_low, gate_mat) + times_transpose(d_up_low, up_mat)
    d_hidden_part, grad_gffin = ffin_pull(d_ffin)
    d_hidden_one = cotangent + d_hidden_part
    d_out_proj, grad_gattn = attn_pull(d_hidden_one)
    d_out_low = d_out_proj.astype(jnp.bfloat16)
    grad_out = transpose_times(mixed_rows, d_out_low)
    d_mixed = (
        times_transpose(d_out_low, out_mat)
        .astype(jnp.bfloat16)
        .reshape(row_count * head_count, head_size)
    )
    probs_full = jnp.exp(masked_scores() - log_total)
    d_probs = times_transpose(d_mixed, value_rows).reshape(row_count, head_count, total_len)
    row_dot = jnp.sum(probs_full * d_probs, axis=-1, keepdims=True)
    d_raw = (
        (probs_full * (d_probs - row_dot) * scaling)
        .astype(jnp.bfloat16)
        .reshape(row_count * head_count, total_len)
    )
    d_queries = matmul(d_raw, key_rows).reshape(row_count, head_count, head_size)
    grad_key_rows = transpose_times(d_raw, query_rows)
    grad_value_rows = transpose_times(probs_low, d_mixed)
    d_keys_own, d_values_own = (
        lax.psum_scatter(
            grad_key_rows.astype(jnp.bfloat16), "seq", scatter_dimension=0, tiled=True
        ).astype(jnp.float32),
        lax.psum_scatter(
            grad_value_rows.astype(jnp.bfloat16), "seq", scatter_dimension=0, tiled=True
        ).astype(jnp.float32),
    )
    d_q_proj, grad_gquery = query_pull(d_queries)
    d_k_proj, grad_gkey = key_pull(d_keys_own)
    d_q_low = d_q_proj.astype(jnp.bfloat16)
    d_k_low = d_k_proj.astype(jnp.bfloat16)
    d_v_low = d_values_own.astype(jnp.bfloat16)
    grad_query = transpose_times(attn_input, d_q_low)
    grad_key = transpose_times(attn_input, d_k_low)
    grad_value = transpose_times(attn_input, d_v_low)
    d_attn_input = (
        times_transpose(d_q_low, query_mat)
        + times_transpose(d_k_low, key_mat)
        + times_transpose(d_v_low, value_mat)
    )
    d_inputs_part, grad_ginput = input_pull(d_attn_input)
    d_inputs = d_hidden_one + d_inputs_part
    shards = (
        lax.psum_scatter(
            grad_query.astype(jnp.bfloat16), "fsdp", scatter_dimension=0, tiled=True
        ).astype(jnp.float32),
        lax.psum_scatter(
            grad_key.astype(jnp.bfloat16), "fsdp", scatter_dimension=0, tiled=True
        ).astype(jnp.float32),
        lax.psum_scatter(
            grad_value.astype(jnp.bfloat16), "fsdp", scatter_dimension=0, tiled=True
        ).astype(jnp.float32),
        lax.psum_scatter(
            grad_out.astype(jnp.bfloat16), "fsdp", scatter_dimension=0, tiled=True
        ).astype(jnp.float32),
        lax.psum_scatter(
            grad_gate.astype(jnp.bfloat16), "fsdp", scatter_dimension=0, tiled=True
        ).astype(jnp.float32),
        lax.psum_scatter(
            grad_up.astype(jnp.bfloat16), "fsdp", scatter_dimension=0, tiled=True
        ).astype(jnp.float32),
        lax.psum_scatter(
            grad_down.astype(jnp.bfloat16), "fsdp", scatter_dimension=0, tiled=True
        ).astype(jnp.float32),
        lax.psum_scatter(
            grad_ginput.astype(jnp.bfloat16), "fsdp", scatter_dimension=0, tiled=True
        ).astype(jnp.float32),
        lax.psum_scatter(
            grad_gquery.astype(jnp.bfloat16), "fsdp", scatter_dimension=0, tiled=True
        ).astype(jnp.float32),
        lax.psum_scatter(
            grad_gkey.astype(jnp.bfloat16), "fsdp", scatter_dimension=0, tiled=True
        ).astype(jnp.float32),
        lax.psum_scatter(
            grad_gattn.astype(jnp.bfloat16), "fsdp", scatter_dimension=0, tiled=True
        ).astype(jnp.float32),
        lax.psum_scatter(
            grad_gffin.astype(jnp.bfloat16), "fsdp", scatter_dimension=0, tiled=True
        ).astype(jnp.float32),
        lax.psum_scatter(
            grad_gffout.astype(jnp.bfloat16), "fsdp", scatter_dimension=0, tiled=True
        ).astype(jnp.float32),
    )
    totals = (
        lax.psum(shards[0].astype(jnp.bfloat16), ("rep", "seq")).astype(jnp.float32),
        lax.psum(shards[1].astype(jnp.bfloat16), ("rep", "seq")).astype(jnp.float32),
        lax.psum(shards[2].astype(jnp.bfloat16), ("rep", "seq")).astype(jnp.float32),
        lax.psum(shards[3].astype(jnp.bfloat16), ("rep", "seq")).astype(jnp.float32),
        lax.psum(shards[4].astype(jnp.bfloat16), ("rep", "seq")).astype(jnp.float32),
        lax.psum(shards[5].astype(jnp.bfloat16), ("rep", "seq")).astype(jnp.float32),
        lax.psum(shards[6].astype(jnp.bfloat16), ("rep", "seq")).astype(jnp.float32),
        lax.psum(shards[7].astype(jnp.bfloat16), ("rep", "seq")).astype(jnp.float32),
        lax.psum(shards[8].astype(jnp.bfloat16), ("rep", "seq")).astype(jnp.float32),
        lax.psum(shards[9].astype(jnp.bfloat16), ("rep", "seq")).astype(jnp.float32),
        lax.psum(shards[10].astype(jnp.bfloat16), ("rep", "seq")).astype(jnp.float32),
        lax.psum(shards[11].astype(jnp.bfloat16), ("rep", "seq")).astype(jnp.float32),
        lax.psum(shards[12].astype(jnp.bfloat16), ("rep", "seq")).astype(jnp.float32),
    )
    return (
        result.astype(jnp.bfloat16)[None],
        d_inputs.astype(jnp.bfloat16)[None],
        totals[0],
        totals[1],
        totals[2],
        totals[3],
        totals[4],
        totals[5],
        totals[6],
        totals[7],
        totals[8],
        totals[9],
        totals[10],
        totals[11],
        totals[12],
    )


def solution(mesh):
    in_specs = (
        P(("rep", "fsdp"), "seq", None),
        P(("rep", "fsdp"), "seq", None),
        P(("rep", "fsdp"), None),
        P("fsdp", None),
        P("fsdp", None),
        P("fsdp", None),
        P("fsdp", None),
        P("fsdp", None),
        P("fsdp", None),
        P("fsdp", None),
        P("fsdp"),
        P("fsdp"),
        P("fsdp"),
        P("fsdp"),
        P("fsdp"),
        P("fsdp"),
    )
    out_specs = (
        P(("rep", "fsdp"), "seq", None),
        P(("rep", "fsdp"), "seq", None),
        P("fsdp", None),
        P("fsdp", None),
        P("fsdp", None),
        P("fsdp", None),
        P("fsdp", None),
        P("fsdp", None),
        P("fsdp", None),
        P("fsdp"),
        P("fsdp"),
        P("fsdp"),
        P("fsdp"),
        P("fsdp"),
        P("fsdp"),
    )
    return jax.shard_map(body, mesh=mesh, in_specs=in_specs, out_specs=out_specs, check_vma=False)
```

profile of v0, /device:TPU:0, one launch (start us, length us, event | category | flops | bytes accessed | tf_op | source)
XLA Modules:
  0.0 610.9 jit_solution(18083511794878233762)
XLA Ops:
  11.2 5.2 all-gather
  16.3 4.2 all-gather.1
  22.8 5.3 all-reduce.17
  29.0 10.0 %all_gather.55 = bf16[640,256]{1,0:T(8,128)(2,1)S(1)} all-gather(bf16[320,256]{1,0:T(8,128)(2,1)S(1)} %copy-done.38), channel_id=1, replica_groups=mesh['rep'=4,'fsdp'=2,'seq'=4] {'fsdp'}, dimensions={0}, use_global_device_ids=true | all-gather | bytes 491520 | tf_op jit(solution)/shard_map/all_gather | solution.py:86
  39.5 6.0 all_gather.58
  45.8 8.1 %all_gather.59 = bf16[1024,256]{1,0:T(8,128)(2,1)} all-gather(bf16[256,256]{1,0:T(8,128)(2,1)S(1)} %convolution_convert_fusion.10), channel_id=1, replica_groups=mesh['rep'=4,'fsdp'=2,'seq'=4] {'seq'}, dimensions={0}, use_global_device_ids=true | all-gather | bytes 655360 | tf_op jit(solution)/shard_map/all_gather | solution.py:137
  54.7 7.3 %all_gather.57 = bf16[1024,256]{0,1:T(8,128)(2,1)S(1)} all-gather(bf16[256,256]{0,1:T(8,128)(2,1)S(1)} %pad_maximum_fusion.3), channel_id=1, replica_groups=mesh['rep'=4,'fsdp'=2,'seq'=4] {'seq'}, dimensions={0}, use_global_device_ids=true | all-gather | bytes 655360 | tf_op jit(solution)/shard_map/all_gather | solution.py:136
  62.0 1.1 fusion.32
  63.1 1.7 copy.54
  66.5 1.0 fusion.102
  67.5 1.0 fusion.2
  68.5 1.0 copy-done
  70.2 1.6 copy.57
  71.9 2.0 reshape.332
  73.9 2.7 convolution_convert_fusion.7
  76.9 2.1 multiply_reduce_fusion.10
  80.6 26.2 %all-gather.12.cloned.1.call-done = bf16[640,2048]{1,0:T(8,128)(2,1)} async-done(((bf16[320,2048]{1,0:T(8,128)(2,1)}), bf16[640,2048]{1,0:T(8,128)(2,1)}) %all-gather.12.cloned.1.call-update) | async-done | bytes 2621456 | tf_op jit(solution)/shard_map/all_gather | solution.py:89
  106.9 4.0 fusion.103
  110.9 36.4 %all-gather.14.cloned.1.call-done = bf16[640,2048]{1,0:T(8,128)(2,1)} async-done(((bf16[320,2048]{1,0:T(8,128)(2,1)}), bf16[640,2048]{1,0:T(8,128)(2,1)}) %all-gather.14.cloned.1.call-update) | async-done | bytes 2621456 | tf_op jit(solution)/shard_map/all_gather | solution.py:90
  147.3 5.2 multiply_convert_fusion.2
  152.6 35.2 %all-gather.16.cloned.1.call-done = bf16[2048,640]{1,0:T(8,128)(2,1)} async-done(((bf16[1024,640]{1,0:T(8,128)(2,1)}), bf16[2048,640]{1,0:T(8,128)(2,1)}) %all-gather.16.cloned.1.call-update) | async-done | bytes 2621456 | tf_op jit(solution)/shard_map/all_gather | solution.py:91
  187.7 3.3 multiply_reduce_fusion.8
  191.9 1.0 fusion.49
  192.9 2.5 multiply_convert_fusion.1
  195.5 1.0 fusion.104
  196.7 1.2 copy-done.10
  197.9 1.7 multiply_reduce_fusion.4
  199.7 1.0 multiply_reduce_fusion.5
  202.2 1.1 reshape.333
  203.3 3.2 convolution_convert_fusion.5
  206.6 3.9 fusion.54
  210.5 12.4 %fusion.27 = bf16[1024,256]{0,1:T(8,128)(2,1)} fusion(f32[256,4,1024]{2,0,1:T(8,128)} %fusion.54, f32[256,4,1024]{2,0,1:T(8,128)} %copy-done, f32[256,4]{0,1:T(4,128)S(1)} %log_add_fusion, bf16[256,4,128]{0,2,1:T(8,128)(2,1)} %copy-done.36, bf16[256,4,128]{0,2,1:T(8,128)(2,1)S(1)} %copy-done.35), kind=kOutput, calls=%fused_computation.34 | convolution fusion | flops 545523712 | bytes 9441280 | tf_op jit(solution)/shard_map/dot_general | solution.py:57
  223.0 5.3 reduce-scatter.12.cloned.1.call-done
  228.4 2.0 convolution_convert_fusion.8
  230.5 22.6 %reduce-scatter.10.cloned.1.call-done = bf16[256,256]{0,1:T(8,128)(2,1)} async-done(((bf16[1024,256]{0,1:T(8,128)(2,1)}), bf16[256,256]{0,1:T(8,128)(2,1)}) %reduce-scatter.10.cloned.1.call-update) | async-done | bytes 131088 | tf_op jit(solution)/shard_map/reduce_scatter | solution.py:210
  253.1 0.9 convert_element_type.252
  255.0 1.1 convolution_convert_fusion.9
  256.2 1.7 convolution_convert_fusion.3
  257.9 10.5 %fusion.9 = f32[256,4,256]{0,2,1:T(8,128)S(1)} fusion(f32[256,4,1024]{2,0,1:T(8,128)} %fusion.54, f32[256,4,1024]{2,0,1:T(8,128)} %copy-done, f32[256,4]{0,1:T(4,128)S(1)} %log_add_fusion, bf16[1024,256]{0,1:T(8,128)(2,1)} %copy-done.33), kind=kOutput, calls=%fused_computation.15 | convolution fusion | flops 544212992 | bytes 9965568 | tf_op jit(solution)/shard_map/dot_general | solution.py:47
  269.0 0.8 multiply_reduce_fusion.1
  270.2 1.7 convolution_convert_fusion.4
  272.0 2.4 convolution_convert_fusion.1
  274.4 1.1 copy-done.29
  275.6 2.4 convolution_convert_fusion.2
  278.0 0.9 copy-done.22
  279.3 2.5 convolution_convert_fusion
  281.9 1.3 reduce-scatter.16.cloned.1.call-done
  283.2 26.0 %reduce-scatter.20.cloned.1.call-done = bf16[512,640]{1,0:T(8,128)(2,1)} async-done(((bf16[1024,640]{1,0:T(8,128)(2,1)}), bf16[512,640]{1,0:T(8,128)(2,1)}) %reduce-scatter.20.cloned.1.call-update) | async-done | bytes 655376 | tf_op jit(solution)/shard_map/reduce_scatter | solution.py:242
  309.2 26.1 %reduce-scatter.14.cloned.1.call-done = bf16[320,1024]{1,0:T(8,128)(2,1)} async-done(((bf16[640,1024]{1,0:T(8,128)(2,1)}), bf16[320,1024]{1,0:T(8,128)(2,1)}) %reduce-scatter.14.cloned.1.call-update) | async-done | bytes 655376 | tf_op jit(solution)/shard_map/reduce_scatter | solution.py:233
  335.3 40.4 %reduce-scatter.24.cloned.1.call-done = bf16[320,2048]{1,0:T(8,128)(2,1)} async-done(((bf16[640,2048]{1,0:T(8,128)(2,1)}), bf16[320,2048]{1,0:T(8,128)(2,1)}) %reduce-scatter.24.cloned.1.call-update) | async-done | bytes 1310736 | tf_op jit(solution)/shard_map/reduce_scatter | solution.py:248
  375.7 40.5 %reduce-scatter.22.cloned.1.call-done = bf16[320,2048]{1,0:T(8,128)(2,1)} async-done(((bf16[640,2048]{1,0:T(8,128)(2,1)}), bf16[320,2048]{1,0:T(8,128)(2,1)}) %reduce-scatter.22.cloned.1.call-update) | async-done | bytes 1310736 | tf_op jit(solution)/shard_map/reduce_scatter | solution.py:245
  416.2 40.4 %reduce-scatter.26.cloned.1.call-done = bf16[1024,640]{1,0:T(8,128)(2,1)} async-done(((bf16[2048,640]{1,0:T(8,128)(2,1)}), bf16[1024,640]{1,0:T(8,128)(2,1)}) %reduce-scatter.26.cloned.1.call-update) | async-done | bytes 1310736 | tf_op jit(solution)/shard_map/reduce_scatter | solution.py:251
  458.8 0.8 fusion.44
  459.6 5.1 all-reduce.16
  465.1 34.6 %all-reduce.14 = (bf16[320]{0:T(512)(128)(2,1)S(1)}, bf16[128]{0:T(256)(128)(2,1)S(1)}, bf16[128]{0:T(256)(128)(2,1)S(1)}, bf16[320]{0:T(512)(128)(2,1)S(1)}, bf...) all-reduce(bf16[320]{0:T(512)(128)(2,1)S(1)} %dynamic-slice.5, ...), channel_id=1, replica_groups=mesh['rep'=4,'fsdp'=2,'seq'=4] {'rep','seq'}, use_global_device_ids=true, to_apply=%region_36.37 | all-reduce | flops 1536 | bytes 6144 | tf_op jit(solution)/shard_map/psum | solution.py:281
  503.1 0.9 fusion.61
  504.0 88.2 %all-reduce.20.cloned.1.call-done = (bf16[320,1024]{1,0:T(8,128)(2,1)}, bf16[320,256]{1,0:T(8,128)(2,1)}, bf16[320,256]{1,0:T(8,128)(2,1)}, bf16[512,640]{1,0:T(...) async-done(((bf16[320,1024]{1,0:T(8,128)(2,1)}, bf16[320,256]{1,0:T(8,128)(2,1)}, bf16[320,256]{1,0:T(8,128)(2,1)}, ...) | async-done | bytes 5570576 | tf_op jit(solution)/shard_map/psum | solution.py:274
  592.2 1.7 convert_element_type.259
  593.9 1.8 convert_element_type.261
  595.7 2.3 convert_element_type.257
  598.0 1.1 convert_element_type.263
  599.2 1.8 convert_element_type.265
  601.0 1.8 convert_element_type.267
  602.8 1.7 convert_element_type.269
  (273 shorter events, 21.6 us)
Async XLA Ops:
  7.2 55.9 %all-gather.8.cloned.1.call-start = ((), (), s32[]{:S(2)}) async-start(), calls=%async_computation.9 | async-start | bytes 1966080 | tf_op jit(solution)/shard_map/all_gather | solution.py:85
  7.9 69.0 %all-gather.10.cloned.1.call-start = ((), (), s32[]{:S(2)}) async-start(), calls=%async_computation.10 | async-start | bytes 1966080 | tf_op jit(solution)/shard_map/all_gather | solution.py:88
  8.7 2.3 copy-start.1
  8.7 2.5 copy-start.83
  8.7 7.6 %copy-start.84 = (bf16[128]{0:T(256)(128)(2,1)S(1)}, bf16[128]{0:T(256)(128)(2,1)}, u32[]{:S(2)}) copy-start(bf16[128]{0:T(256)(128)(2,1)} %param.28) | copy-start | bytes 772
  8.7 11.9 %copy-start.74 = (u32[32]{0:T(128)S(1)}, u32[32]{0:T(128)}, u32[]{:S(2)}) copy-start(u32[32]{0:T(128)} %constant.76) | copy-start | bytes 388
  8.7 13.1 %copy-start.77 = (bf16[320]{0:T(512)(128)(2,1)S(1)}, bf16[320]{0:T(512)(128)(2,1)}, u32[]{:S(2)}) copy-start(bf16[320]{0:T(512)(128)(2,1)} %param.30) | copy-start | bytes 1924
  8.7 13.4 %copy-start.78 = (bf16[320]{0:T(512)(128)(2,1)S(1)}, bf16[320]{0:T(512)(128)(2,1)}, u32[]{:S(2)}) copy-start(bf16[320]{0:T(512)(128)(2,1)} %param.29) | copy-start | bytes 1924
  8.7 13.6 %copy-start.79 = (bf16[320]{0:T(512)(128)(2,1)S(1)}, bf16[320]{0:T(512)(128)(2,1)}, u32[]{:S(2)}) copy-start(bf16[320]{0:T(512)(128)(2,1)} %param.26) | copy-start | bytes 1924
  8.7 13.8 %copy-start.80 = (bf16[320]{0:T(512)(128)(2,1)S(1)}, bf16[320]{0:T(512)(128)(2,1)}, u32[]{:S(2)}) copy-start(bf16[320]{0:T(512)(128)(2,1)} %param.31) | copy-start | bytes 1924
  8.8 20.3 %copy-start.38 = (bf16[320,256]{1,0:T(8,128)(2,1)S(1)}, bf16[320,256]{1,0:T(8,128)(2,1)}, u32[]{:S(2)}) copy-start(bf16[320,256]{1,0:T(8,128)(2,1)} %param.20) | copy-start | bytes 491524
  8.8 98.1 %all-gather.12.cloned.1.call-start = ((), (), s32[]{:S(2)}) async-start(), calls=%async_computation.11 | async-start | bytes 3932160 | tf_op jit(solution)/shard_map/all_gather | solution.py:89
  9.5 30.0 %copy-start.39 = (bf16[320,256]{1,0:T(8,128)(2,1)S(1)}, bf16[320,256]{1,0:T(8,128)(2,1)}, u32[]{:S(2)}) copy-start(bf16[320,256]{1,0:T(8,128)(2,1)} %param.21) | copy-start | bytes 491524
  9.5 137.8 %all-gather.14.cloned.1.call-start = ((), (), s32[]{:S(2)}) async-start(), calls=%async_computation.12 | async-start | bytes 3932160 | tf_op jit(solution)/shard_map/all_gather | solution.py:90
  10.1 177.6 %all-gather.16.cloned.1.call-start = ((), (), s32[]{:S(2)}) async-start(), calls=%async_computation.13 | async-start | bytes 3932160 | tf_op jit(solution)/shard_map/all_gather | solution.py:91
  10.7 217.7 %reduce-scatter.12.cloned.1.call-start = ((), (), s32[]{:S(2)}) async-start(), calls=%async_computation.15 | async-start | bytes 655360 | tf_op jit(solution)/shard_map/reduce_scatter | solution.py:213
  10.8 43.3 %copy-start.75 = (f32[128]{0:T(128)}, f32[128]{0:T(128)S(1)}, u32[]{:S(2)}) copy-start(f32[128]{0:T(128)S(1)} %multiply_power_fusion) | copy-start | bytes 1540
  11.1 42.9 %copy-start.62 = (f32[256]{0:T(256)}, f32[256]{0:T(256)S(1)}, u32[]{:S(2)}) copy-start(f32[256]{0:T(256)S(1)} %fusion.45) | copy-start | bytes 3076
  11.1 53.7 %copy-start.48 = (f32[256]{0:T(256)}, f32[256]{0:T(256)S(1)}, u32[]{:S(2)}) copy-start(f32[256]{0:T(256)S(1)} %fusion.83) | copy-start | bytes 3076
  16.3 49.2 %copy-start.52 = (f32[2,1,128]{2,1,0:T(1,128)}, f32[2,1,128]{2,1,0:T(1,128)S(1)}, u32[]{:S(2)}) copy-start(f32[2,1,128]{2,1,0:T(1,128)S(1)} %convert_element_type.284) | copy-start | bytes 3076
  20.6 33.5 %copy-start.54 = (f32[2,1,128]{2,1,0:T(1,128)}, f32[2,1,128]{2,1,0:T(1,128)S(1)}, u32[]{:S(2)}) copy-start(f32[2,1,128]{2,1,0:T(1,128)S(1)} %convert_element_type.285) | copy-start | bytes 3076
  28.4 26.2 %copy-start.60 = (f32[256]{0:T(256)}, f32[256]{0:T(256)S(1)}, u32[]{:S(2)}) copy-start(f32[256]{0:T(256)S(1)} %dynamic-slice_convert_fusion) | copy-start | bytes 3076
  39.0 15.6 %copy-start.17 = (bf16[640,256]{1,0:T(8,128)(2,1)}, bf16[640,256]{1,0:T(8,128)(2,1)S(1)}, u32[]{:S(2)}) copy-start(bf16[640,256]{1,0:T(8,128)(2,1)S(1)} %all_gather.55) | copy-start | bytes 983044
  39.4 22.6 %copy-start.11 = (f32[256,256]{0,1:T(8,128)}, f32[256,256]{0,1:T(8,128)S(1)}, u32[]{:S(2)}) copy-start(f32[256,256]{0,1:T(8,128)S(1)} %get-tuple-element.72) | copy-start | bytes 786436
  39.4 22.6 %copy-start.71 = (f32[256]{0:T(256)}, f32[256]{0:T(256)S(1)}, u32[]{:S(2)}) copy-start(f32[256]{0:T(256)S(1)} %get-tuple-element.71) | copy-start | bytes 3076
  39.5 22.5 %copy-start.56 = (f32[256]{0:T(256)}, f32[256]{0:T(256)S(1)}, u32[]{:S(2)}) copy-start(f32[256]{0:T(256)S(1)} %fusion.84) | copy-start | bytes 3076
  45.5 9.2 %copy-start.19 = (bf16[640,256]{1,0:T(8,128)(2,1)}, bf16[640,256]{1,0:T(8,128)(2,1)S(1)}, u32[]{:S(2)}) copy-start(bf16[640,256]{1,0:T(8,128)(2,1)S(1)} %all_gather.58) | copy-start | bytes 983044
  54.7 11.1 %copy-start.23 = (f32[256,128]{0,1:T(8,128)}, f32[256,128]{0,1:T(8,128)S(1)}, u32[]{:S(2)}) copy-start(f32[256,128]{0,1:T(8,128)S(1)} %get-tuple-element.65) | copy-start | bytes 393220
  54.7 11.1 %copy-start.25 = (f32[256,128]{0,1:T(8,128)}, f32[256,128]{0,1:T(8,128)S(1)}, u32[]{:S(2)}) copy-start(f32[256,128]{0,1:T(8,128)S(1)} %get-tuple-element.66) | copy-start | bytes 393220
  62.0 3.9 copy-start.33
  187.7 3.3 copy-start.8
  187.7 3.3 copy-start.41
  187.7 5.1 copy-start.81
  187.7 5.1 copy-start.85
  192.9 2.5 copy-start.21
  192.9 2.6 copy-start.9
  195.4 2.5 copy-start.10
  195.5 2.5 copy-start.59
  203.3 3.3 copy-start.45
  203.3 3.3 copy-start.47
  206.5 46.6 %reduce-scatter.10.cloned.1.call-start = ((), (), s32[]{:S(2)}) async-start(), calls=%async_computation.14 | async-start | bytes 655360 | tf_op jit(solution)/shard_map/reduce_scatter | solution.py:210
  206.6 3.9 copy-start.35
  210.5 17.9 %copy-start.49 = (f32[256]{0:T(256)S(1)}, f32[256]{0:T(256)}, u32[]{:S(2)}) copy-start(f32[256]{0:T(256)} %copy-done.48) | copy-start | bytes 3076
  222.9 31.1 %copy-start.61 = (f32[256]{0:T(256)S(1)}, f32[256]{0:T(256)}, u32[]{:S(2)}) copy-start(f32[256]{0:T(256)} %copy-done.60) | copy-start | bytes 3076
  222.9 31.1 %copy-start.76 = (f32[128]{0:T(128)S(1)}, f32[128]{0:T(128)}, u32[]{:S(2)}) copy-start(f32[128]{0:T(128)} %copy-done.75) | copy-start | bytes 1540
  222.9 31.7 %copy-start.12 = (f32[256,256]{0,1:T(8,128)S(1)}, f32[256,256]{0,1:T(8,128)}, u32[]{:S(2)}) copy-start(f32[256,256]{0,1:T(8,128)} %copy-done.11) | copy-start | bytes 786436
  222.9 31.7 %copy-start.55 = (f32[2,1,128]{2,1,0:T(1,128)S(1)}, f32[2,1,128]{2,1,0:T(1,128)}, u32[]{:S(2)}) copy-start(f32[2,1,128]{2,1,0:T(1,128)} %copy-done.54) | copy-start | bytes 3076
  222.9 31.7 %copy-start.57 = (f32[256]{0:T(256)S(1)}, f32[256]{0:T(256)}, u32[]{:S(2)}) copy-start(f32[256]{0:T(256)} %copy-done.56) | copy-start | bytes 3076
  222.9 31.9 %copy-start.72 = (f32[256]{0:T(256)S(1)}, f32[256]{0:T(256)}, u32[]{:S(2)}) copy-start(f32[256]{0:T(256)} %copy-done.71) | copy-start | bytes 3076
  223.0 58.9 %reduce-scatter.18.cloned.1.call-start = ((), (), s32[]{:S(2)}) async-start(), calls=%async_computation.18 | async-start | bytes 491520 | tf_op jit(solution)/shard_map/reduce_scatter | solution.py:239
  230.4 52.8 %reduce-scatter.16.cloned.1.call-start = ((), (), s32[]{:S(2)}) async-start(), calls=%async_computation.17 | async-start | bytes 491520 | tf_op jit(solution)/shard_map/reduce_scatter | solution.py:236
  255.0 2.9 copy-start.31
  256.1 53.0 %reduce-scatter.20.cloned.1.call-start = ((), (), s32[]{:S(2)}) async-start(), calls=%async_computation.19 | async-start | bytes 1966080 | tf_op jit(solution)/shard_map/reduce_scatter | solution.py:242
  257.9 10.5 %copy-start.24 = (f32[256,128]{0,1:T(8,128)S(1)}, f32[256,128]{0,1:T(8,128)}, u32[]{:S(2)}) copy-start(f32[256,128]{0,1:T(8,128)} %copy-done.23) | copy-start | bytes 393220
  257.9 10.5 %copy-start.26 = (f32[256,128]{0,1:T(8,128)S(1)}, f32[256,128]{0,1:T(8,128)}, u32[]{:S(2)}) copy-start(f32[256,128]{0,1:T(8,128)} %copy-done.25) | copy-start | bytes 393220
  257.9 77.4 %reduce-scatter.14.cloned.1.call-start = ((), (), s32[]{:S(2)}) async-start(), calls=%async_computation.16 | async-start | bytes 1966080 | tf_op jit(solution)/shard_map/reduce_scatter | solution.py:233
  271.9 103.7 %reduce-scatter.24.cloned.1.call-start = ((), (), s32[]{:S(2)}) async-start(), calls=%async_computation.21 | async-start | bytes 3932160 | tf_op jit(solution)/shard_map/reduce_scatter | solution.py:248
  274.4 141.8 %reduce-scatter.22.cloned.1.call-start = ((), (), s32[]{:S(2)}) async-start(), calls=%async_computation.20 | async-start | bytes 3932160 | tf_op jit(solution)/shard_map/reduce_scatter | solution.py:245
  278.0 178.6 %reduce-scatter.26.cloned.1.call-start = ((), (), s32[]{:S(2)}) async-start(), calls=%async_computation.22 | async-start | bytes 3932160 | tf_op jit(solution)/shard_map/reduce_scatter | solution.py:251
  281.8 310.4 %all-reduce.20.cloned.1.call-start = ((), (), s32[]{:S(2)}) async-start(), calls=%async_computation.23 | async-start | bytes 11141120 | tf_op jit(solution)/shard_map/psum | solution.py:274
  458.8 44.3 %copy-start.63 = (f32[256]{0:T(256)S(1)}, f32[256]{0:T(256)}, u32[]{:S(2)}) copy-start(f32[256]{0:T(256)} %copy-done.62) | copy-start | bytes 3076
  458.8 44.3 %copy-start.3 = (f32[256,640]{1,0:T(8,128)S(1)}, f32[256,640]{1,0:T(8,128)}, u32[]{:S(2)}) copy-start(f32[256,640]{1,0:T(8,128)} %copy-done.2) | copy-start | bytes 1966084
  592.2 5.8 copy-start.30
  593.9 5.2 copy-start.16
  (37 other events, 49.8 us)
Sparse Core Ops, SparseCore 0:
  9.5 31.1 all-gather.7
  42.2 24.0 all-gather.9
  67.8 38.9 all-gather.11
  108.3 38.9 all-gather.13
  148.7 38.9 all-gather.15
  206.7 21.6 reduce-scatter.11
  231.4 21.6 reduce-scatter.9
  255.3 12.4 reduce-scatter.17
  270.7 12.4 reduce-scatter.15
  285.8 23.2 reduce-scatter.19
  312.0 23.2 reduce-scatter.13
  338.0 37.6 reduce-scatter.23
  378.5 37.6 reduce-scatter.21
  418.9 37.6 reduce-scatter.25
  461.1 131.0 all-reduce.19
where the time goes:
time: 612 us; the launch traced here: 611 us
  waiting for transfers between devices  392 us (64%)
  blocking collectives  85.7 us (14%)
  matrix products  70.8 us (12%)
  other arithmetic  28 us (5%)
  between operations  17.2 us (3%)
  local copies, waits for them, and re-layouts  16.7 us (3%)
    psum x1, waiting for transfers between devices, body(): lax.psum(shards[0].astype(jnp.bfloat16), ('rep', 'seq')).astype(jnp.float32)  88.2 us
    reduce_scatter x1, waiting for transfers between devices, body(): lax.psum_scatter(grad_gate.astype(jnp.bfloat16), 'fsdp', scatter_dimensio...  40.5 us
    reduce_scatter x1, waiting for transfers between devices, body(): lax.psum_scatter(grad_down.astype(jnp.bfloat16), 'fsdp', scatter_dimensio...  40.4 us
    reduce_scatter x1, waiting for transfers between devices, body(): lax.psum_scatter(grad_up.astype(jnp.bfloat16), 'fsdp', scatter_dimension=...  40.4 us
    all_gather x1, waiting for transfers between devices, body(): lax.all_gather(w_up, 'fsdp', axis=0, tiled=True)  36.4 us
    all_gather x1, waiting for transfers between devices, body(): lax.all_gather(w_down, 'fsdp', axis=0, tiled=True)  35.2 us
    psum x1, blocking collectives, body(): lax.psum(shards[7].astype(jnp.bfloat16), ('rep', 'seq')).astype(jnp.float32)  34.6 us
    dot_general x9, matrix products, transpose_times(): lax.dot_general(left_side, right_side, (((0,), (0,)), ((), ())), preferre...  29.4 us
  transfers between devices with their start and end apart: 15, of which 12 were waited for; matrix products, arithmetic and copies ran while one was open for 13% of the time, Pallas kernels for 0%

commit v1 on v0

v1 whole, which is shorter than its diff:
```python
import jax
import jax.numpy as jnp
from jax import lax
from jax.sharding import PartitionSpec as P

EPS = 1e-06
ROPE_BASE = 1000000.0
MASKED = -1e30


def rms_norm(values, gain_vec):
    return values * lax.rsqrt(jnp.mean(values * values, axis=-1, keepdims=True) + EPS) * gain_vec


def rotate(values, angles):
    half_width = values.shape[-1] // 2
    front_half = values[..., :half_width]
    back_half = values[..., half_width:]
    cos_part = jnp.cos(angles)
    sin_part = jnp.sin(angles)
    return jnp.concatenate(
        [
            front_half * cos_part - back_half * sin_part,
            back_half * cos_part + front_half * sin_part,
        ],
        axis=-1,
    )


def frequencies(head_size):
    return jnp.power(
        jnp.float32(ROPE_BASE), -2.0 * jnp.arange(head_size // 2, dtype=jnp.float32) / head_size
    )


def layout(lengths_row, total_len):
    doc_ends = jnp.cumsum(lengths_row)
    starts = doc_ends - lengths_row
    indices = jnp.arange(total_len, dtype=jnp.int32)
    segment = jnp.sum((indices[:, None] >= doc_ends[None, :]).astype(jnp.int32), axis=1)
    onehot = segment[:, None] == jnp.arange(lengths_row.shape[0], dtype=jnp.int32)[None, :]
    doc_begin = jnp.sum(jnp.where(onehot, starts[None, :], 0), axis=1)
    return (segment, indices - doc_begin)


def matmul(left_side, right_side):
    return jnp.dot(left_side, right_side, preferred_element_type=jnp.float32)


def times_transpose(left_side, right_side):
    return lax.dot_general(
        left_side, right_side, (((1,), (1,)), ((), ())), preferred_element_type=jnp.float32
    )


def transpose_times(left_side, right_side):
    return lax.dot_general(
        left_side, right_side, (((0,), (0,)), ((), ())), preferred_element_type=jnp.float32
    )


def gated(gate_proj, up_proj):
    return jax.nn.gelu(gate_proj, approximate=True) * up_proj


def swap(values, axis_name, bit):
    size = lax.axis_size(axis_name)
    return lax.ppermute(values, axis_name, [(i, i ^ bit) for i in range(size)])


def halve(values, axis_name, bit, dim):
    mine = (lax.axis_index(axis_name) // bit) % 2
    sent = lax.dynamic_index_in_dim(values, 1 - mine, dim, keepdims=False)
    kept = lax.dynamic_index_in_dim(values, mine, dim, keepdims=False)
    arrived = swap(sent, axis_name, bit)
    return (kept.astype(jnp.float32) + arrived.astype(jnp.float32)).astype(jnp.bfloat16)


def paired():
    return lax.axis_size("fsdp") == 2 and lax.axis_size("seq") == 4


def gather_rows(shard):
    if not paired():
        return lax.all_gather(shard, "fsdp", axis=0, tiled=True)
    rows = shard.shape[0] // 4
    piece = lax.dynamic_slice_in_dim(shard, lax.axis_index("seq") * rows, rows)
    other = lax.all_gather(swap(piece, "fsdp", 1), "seq", axis=0, tiled=True)
    first = lax.axis_index("fsdp") == 0
    return jnp.concatenate([jnp.where(first, shard, other), jnp.where(first, other, shard)], axis=0)


def reduce_blocks(blocks, across_first, before):
    _, _, rows, columns = blocks.shape
    part = blocks.reshape(2, 2, 2, rows, columns)
    part = halve(part, "seq", 1, 2)
    if across_first:
        part = halve(part, "fsdp", 1, 0)
        part = halve(part, "seq", 2, 0)
    else:
        part = halve(part, "seq", 2, 1)
        part = halve(part, "fsdp", 1, 0)
    if before is not None:
        part, _ = lax.optimization_barrier((part, before))
    part = lax.psum(part, "rep")
    return lax.all_gather(part, "seq", axis=0, tiled=True).reshape(4, rows, columns), part


def reduce_rows(grad, across_first, before):
    low = grad.astype(jnp.bfloat16)
    if not paired():
        own = lax.psum_scatter(low, "fsdp", scatter_dimension=0, tiled=True)
        return lax.psum(own, ("rep", "seq")).astype(jnp.float32), None
    rows, columns = low.shape
    own, last = reduce_blocks(low.reshape(2, 4, rows // 8, columns), across_first, before)
    return own.reshape(rows // 2, columns).astype(jnp.float32), last


def reduce_with_gains(grad, gains, before):
    width = gains.shape[1]
    rows, columns = grad.shape
    if not paired() or width > columns:
        own = lax.psum_scatter(
            gains.astype(jnp.bfloat16), "fsdp", scatter_dimension=0, tiled=True
        )
        own = lax.psum(own, ("rep", "seq")).astype(jnp.float32)
        return reduce_rows(grad, True, before)[0], own[0]
    extra = jnp.pad(
        gains.astype(jnp.bfloat16)[:, None, None, :],
        ((0, 0), (0, 3), (0, 15), (0, columns - width)),
    )
    blocks = jnp.concatenate(
        [grad.astype(jnp.bfloat16).reshape(2, 4, rows // 8, columns), extra], axis=2
    )
    own, _ = reduce_blocks(blocks, True, before)
    matrix = own[:, : rows // 8].reshape(rows // 2, columns).astype(jnp.float32)
    return matrix, own[0, rows // 8, :width].astype(jnp.float32)


def body(
    tokens,
    d_out,
    doc_lengths,
    w_query,
    w_key,
    w_value,
    w_out,
    w_gate,
    w_up,
    w_down,
    g_input,
    g_query,
    g_key,
    g_attn,
    g_ffin,
    g_ffout,
):
    shards = lax.axis_size("fsdp")
    gain_shards = (g_input, g_query, g_key, g_attn, g_ffin, g_ffout)
    widths = [entry.shape[0] for entry in gain_shards]
    starts = [sum(widths[:i]) for i in range(len(widths))]
    gain_rows = lax.all_gather(jnp.concatenate(gain_shards)[None], "fsdp", axis=0, tiled=True)
    gain_input, gain_query, gain_key, gain_attn, gain_ffin, gain_ffout = [
        gain_rows[:, at : at + width].reshape(-1).astype(jnp.float32)
        for at, width in zip(starts, widths)
    ]
    qkv_mat = gather_rows(jnp.concatenate([w_query, w_key, w_value], axis=1))
    out_mat = gather_rows(w_out)
    gate_up_mat = gather_rows(jnp.concatenate([w_gate, w_up], axis=1))
    down_mat = gather_rows(w_down)
    row_count = tokens.shape[1]
    head_size = gain_query.shape[0]
    query_width = w_query.shape[1]
    head_count = query_width // head_size
    ff_width = w_gate.shape[1]
    total_len = row_count * lax.axis_size("seq")
    segment, position = layout(doc_lengths[0], total_len)
    offset = lax.axis_index("seq") * row_count
    query_seg = lax.dynamic_slice_in_dim(segment, offset, row_count)
    query_pos = lax.dynamic_slice_in_dim(position, offset, row_count)
    places = offset + jnp.arange(row_count, dtype=jnp.int32)
    allowed = (query_seg[:, None] == segment[None, :]) & (
        places[:, None] >= jnp.arange(total_len, dtype=jnp.int32)[None, :]
    )
    angles = query_pos.astype(jnp.float32)[:, None] * frequencies(head_size)[None, :]
    scaling = head_size ** (-0.5)
    inputs = tokens[0].astype(jnp.float32)
    cotangent = d_out[0].astype(jnp.float32)
    input_norm, input_pull = jax.vjp(rms_norm, inputs, gain_input)
    attn_input = input_norm.astype(jnp.bfloat16)
    qkv_proj = matmul(attn_input, qkv_mat)
    q_proj = qkv_proj[:, :query_width]
    k_proj = qkv_proj[:, query_width : query_width + head_size]
    v_proj = qkv_proj[:, query_width + head_size :]

    def query_fn(projected, gain_vec):
        shaped = projected.reshape(projected.shape[0], -1, gain_vec.shape[0])
        return rotate(rms_norm(shaped, gain_vec), angles[:, None, :])

    def key_fn(projected, gain_vec):
        return rotate(rms_norm(projected, gain_vec), angles)

    queries, query_pull = jax.vjp(query_fn, q_proj, gain_query)
    keys_own, key_pull = jax.vjp(key_fn, k_proj, gain_key)
    query_rows = queries.astype(jnp.bfloat16).reshape(row_count * head_count, head_size)
    key_value_rows = lax.all_gather(
        jnp.concatenate([keys_own.astype(jnp.bfloat16), v_proj.astype(jnp.bfloat16)], axis=1),
        "seq",
        axis=0,
        tiled=True,
    )
    key_rows = key_value_rows[:, :head_size]
    value_rows = key_value_rows[:, head_size:]

    def masked_scores():
        raw_scores = times_transpose(query_rows, key_rows).reshape(row_count, head_count, total_len)
        return jnp.where(allowed[:, None, :], raw_scores * scaling, MASKED)

    scores = masked_scores()
    top_score = jnp.max(scores, axis=-1, keepdims=True)
    shifted = jnp.exp(scores - top_score)
    denominator = jnp.sum(shifted, axis=-1, keepdims=True)
    log_total = top_score + jnp.log(denominator)
    probs_low = (
        (shifted / denominator).astype(jnp.bfloat16).reshape(row_count * head_count, total_len)
    )
    mixed_rows = (
        matmul(probs_low, value_rows)
        .reshape(row_count, head_count * head_size)
        .astype(jnp.bfloat16)
    )
    out_proj = matmul(mixed_rows, out_mat)
    attn_norm, attn_pull = jax.vjp(rms_norm, out_proj, gain_attn)
    hidden_one = inputs + attn_norm
    ffin_norm, ffin_pull = jax.vjp(rms_norm, hidden_one, gain_ffin)
    ff_input = ffin_norm.astype(jnp.bfloat16)
    gate_up_proj = matmul(ff_input, gate_up_mat)
    gate_proj = gate_up_proj[:, :ff_width]
    up_proj = gate_up_proj[:, ff_width:]
    activated, gated_pull = jax.vjp(gated, gate_proj, up_proj)
    hidden = activated.astype(jnp.bfloat16)
    down_proj = matmul(hidden, down_mat)
    ffout_norm, ffout_pull = jax.vjp(rms_norm, down_proj, gain_ffout)
    result = hidden_one + ffout_norm
    d_down, grad_gffout = ffout_pull(cotangent)
    d_down_low = d_down.astype(jnp.bfloat16)
    total_down, last = reduce_rows(transpose_times(hidden, d_down_low), True, None)
    d_hidden = times_transpose(d_down_low, down_mat)
    d_gate, d_up = gated_pull(d_hidden)
    d_gate_up_low = jnp.concatenate(
        [d_gate.astype(jnp.bfloat16), d_up.astype(jnp.bfloat16)], axis=1
    )
    total_gate_up, last = reduce_rows(transpose_times(ff_input, d_gate_up_low), False, last)
    d_ffin = times_transpose(d_gate_up_low, gate_up_mat)
    d_hidden_part, grad_gffin = ffin_pull(d_ffin)
    d_hidden_one = cotangent + d_hidden_part
    d_out_proj, grad_gattn = attn_pull(d_hidden_one)
    d_out_low = d_out_proj.astype(jnp.bfloat16)
    total_out, last = reduce_rows(transpose_times(mixed_rows, d_out_low), True, last)
    d_mixed = (
        times_transpose(d_out_low, out_mat)
        .astype(jnp.bfloat16)
        .reshape(row_count * head_count, head_size)
    )
    probs_full = jnp.exp(masked_scores() - log_total)
    d_probs = times_transpose(d_mixed, value_rows).reshape(row_count, head_count, total_len)
    row_dot = jnp.sum(probs_full * d_probs, axis=-1, keepdims=True)
    d_raw = (
        (probs_full * (d_probs - row_dot) * scaling)
        .astype(jnp.bfloat16)
        .reshape(row_count * head_count, total_len)
    )
    grad_rows = jnp.concatenate(
        [
            transpose_times(d_raw, query_rows).astype(jnp.bfloat16),
            transpose_times(probs_low, d_mixed).astype(jnp.bfloat16),
        ],
        axis=1,
    )
    d_queries = matmul(d_raw, key_rows).reshape(row_count, head_count, head_size)
    if paired():
        grad_own = grad_rows.reshape(2, 2, row_count, 2 * head_size)
        grad_own = halve(halve(grad_own, "seq", 1, 1), "seq", 2, 0).astype(jnp.float32)
    else:
        grad_own = lax.psum_scatter(
            grad_rows, "seq", scatter_dimension=0, tiled=True
        ).astype(jnp.float32)
    d_q_proj, grad_gquery = query_pull(d_queries)
    d_k_proj, grad_gkey = key_pull(grad_own[:, :head_size])
    d_qkv_low = jnp.concatenate(
        [
            d_q_proj.astype(jnp.bfloat16),
            d_k_proj.astype(jnp.bfloat16),
            grad_own[:, head_size:].astype(jnp.bfloat16),
        ],
        axis=1,
    )
    d_qkv_low, last, total_down = lax.optimization_barrier((d_qkv_low, last, total_down))
    grad_qkv = transpose_times(attn_input, d_qkv_low)
    d_attn_input = times_transpose(d_qkv_low, qkv_mat)
    d_inputs_part, grad_ginput = input_pull(d_attn_input)
    d_inputs = d_hidden_one + d_inputs_part
    grad_gains = (grad_ginput, grad_gquery, grad_gkey, grad_gattn, grad_gffin, grad_gffout)
    packed_gains = jnp.concatenate([entry.reshape(shards, -1) for entry in grad_gains], axis=1)
    total_qkv, total_gains = reduce_with_gains(grad_qkv, packed_gains, last)
    return (
        result.astype(jnp.bfloat16)[None],
        d_inputs.astype(jnp.bfloat16)[None],
        total_qkv[:, :query_width],
        total_qkv[:, query_width : query_width + head_size],
        total_qkv[:, query_width + head_size :],
        total_out,
        total_gate_up[:, :ff_width],
        total_gate_up[:, ff_width:],
        total_down,
    ) + tuple(total_gains[at : at + width] for at, width in zip(starts, widths))


def solution(mesh):
    in_specs = (
        P(("rep", "fsdp"), "seq", None),
        P(("rep", "fsdp"), "seq", None),
        P(("rep", "fsdp"), None),
        P("fsdp", None),
        P("fsdp", None),
        P("fsdp", None),
        P("fsdp", None),
        P("fsdp", None),
        P("fsdp", None),
        P("fsdp", None),
        P("fsdp"),
        P("fsdp"),
        P("fsdp"),
        P("fsdp"),
        P("fsdp"),
        P("fsdp"),
    )
    out_specs = (
        P(("rep", "fsdp"), "seq", None),
        P(("rep", "fsdp"), "seq", None),
        P("fsdp", None),
        P("fsdp", None),
        P("fsdp", None),
        P("fsdp", None),
        P("fsdp", None),
        P("fsdp", None),
        P("fsdp", None),
        P("fsdp"),
        P("fsdp"),
        P("fsdp"),
        P("fsdp"),
        P("fsdp"),
        P("fsdp"),
    )
    return jax.shard_map(body, mesh=mesh, in_specs=in_specs, out_specs=out_specs, check_vma=False)
```

time: 612 us -> 470 us (0.77); the launches traced: 611 us -> 462 us
  waiting for transfers between devices: 392 us -> 242 us
  blocking collectives: 85.7 us -> 30.1 us
  local copies, waits for them, and re-layouts: 16.7 us -> 50.4 us
  other arithmetic: 28 us -> 47.8 us
  starting transfers between devices: 0.6 us -> 18.4 us
  matrix products: 70.8 us -> 57.5 us
    reduce_scatter x9 -> x0, waiting for transfers between devices: 203 us -> none  [the longest x1 40.5 us: body(): lax.psum_scatter(grad_gate.astype(jnp.bfloat16), 'fsdp', scatter_dimensio...]
    ppermute x0 -> x18, waiting for transfers between devices: none -> 62.7 us  [swap(): return lax.ppermute(values, axis_name, [(i, i ^ bit) for i in range(size)])]
    all_gather x5 -> x6, waiting for transfers between devices: 97.8 us -> 60 us  [the longest x3 49 us: reduce_blocks(): lax.all_gather(part, 'seq', axis=0, tiled=True).reshape(4, rows, columns)]
    psum x1 -> x0, blocking collectives: 34.6 us -> none  [body(): lax.psum(shards[7].astype(jnp.bfloat16), ('rep', 'seq')).astype(jnp.float32)]
    psum x1 -> x4, waiting for transfers between devices: 88.2 us -> 118 us  [reduce_blocks(): part = lax.psum(part, 'rep')]
    ppermute x0 -> x18, starting transfers between devices: none -> 18 us  [swap(): return lax.ppermute(values, axis_name, [(i, i ^ bit) for i in range(size)])]
    all_gather x6 -> x4, blocking collectives: 40.8 us -> 30.1 us  [the longest x2 16.8 us: gather_rows(): other = lax.all_gather(swap(piece, 'fsdp', 1), 'seq', axis=0, tiled=True)]
    unnamed x2 -> x0, blocking collectives: 10.3 us -> none
  transfers between devices with their start and end apart: 15 -> 28, of which waited for: 12 -> 19; matrix products, arithmetic and copies ran while one was open for 13% -> 23% of each run, Pallas kernels for 0% -> 0%
where the time goes in v1:
time: 470 us; the launch traced here: 462 us
  waiting for transfers between devices  242 us (51%)
  matrix products  57.5 us (12%)
  local copies, waits for them, and re-layouts  50.4 us (11%)
  other arithmetic  47.8 us (10%)
  blocking collectives  30.1 us (6%)
  starting transfers between devices  18.4 us (4%)
  between operations  15.6 us (3%)
    psum x4, waiting for transfers between devices, reduce_blocks(): part = lax.psum(part, 'rep')  118 us
    ppermute x18, waiting for transfers between devices, swap(): return lax.ppermute(values, axis_name, [(i, i ^ bit) for i in range(size)])  62.7 us
    all_gather x3, waiting for transfers between devices, reduce_blocks(): lax.all_gather(part, 'seq', axis=0, tiled=True).reshape(4, rows, columns)  49 us
    dot_general x6, matrix products, transpose_times(): lax.dot_general(left_side, right_side, (((0,), (0,)), ((), ())), preferre...  21.6 us
    dot_general x6, matrix products, matmul(): return jnp.dot(left_side, right_side, preferred_element_type=jnp.float32)  20.7 us
    ppermute x18, starting transfers between devices, swap(): return lax.ppermute(values, axis_name, [(i, i ^ bit) for i in range(size)])  18 us
    all_gather x2, blocking collectives, gather_rows(): other = lax.all_gather(swap(piece, 'fsdp', 1), 'seq', axis=0, tiled=True)  16.8 us
    convert_element_type x13, other arithmetic, halve(): (kept.astype(jnp.float32) + arrived.astype(jnp.float32)).astype(jnp.bfloa...  15.9 us
  transfers between devices with their start and end apart: 28, of which 19 were waited for; matrix products, arithmetic and copies ran while one was open for 23% of the time, Pallas kernels for 0%

profile of v1, /device:TPU:0, one launch (start us, length us, event | category | flops | bytes accessed | tf_op | source)
XLA Modules:
  0.0 461.8 jit_solution(1109950288446582475)
XLA Ops:
  10.4 3.0 collective-permute-start
  14.1 5.5 %all-gather.1 = bf16[2,1,1536]{2,1,0:T(2,128)(2,1)S(1)} all-gather(bf16[1,1,1536]{2,1,0:T(2,128)(2,1)S(1)} %reshape.530), channel_id=2, replica_groups=mesh['rep'=4,'fsdp'=2,'seq'=4] {'fsdp'}, dimensions={0}, use_global_device_ids=true | all-gather | bytes 9216 | tf_op jit(solution)/shard_map/all_gather | solution.py:162
  20.0 9.9 %all_gather.31 = bf16[320,1536]{1,0:T(8,128)(2,1)S(1)} all-gather(bf16[80,1536]{1,0:T(8,128)(2,1)S(1)} %collective-permute-done), channel_id=1, replica_groups=mesh['rep'=4,'fsdp'=2,'seq'=4] {'seq'}, dimensions={0}, use_global_device_ids=true | all-gather | bytes 1228800 | tf_op jit(solution)/shard_map/all_gather | solution.py:88
  33.0 1.7 constant_dynamic-slice_fusion.2
  34.8 1.5 collective-permute-start.3
  36.3 8.7 %collective-permute-done.3 = bf16[256,640]{1,0:T(8,128)(2,1)S(1)} collective-permute-done((bf16[256,640]{1,0:T(8,128)(2,1)}, bf16[256,640]{1,0:T(8,128)(2,1)S(1)}, u32[]{:S(2)}, u32[]{:S(2)}) %collective-permute-start.3) | collective-permute-done | bytes 327712 | tf_op jit(solution)/shard_map/ppermute | solution.py:68
  45.8 1.6 collective-permute-start.1
  50.3 1.5 copy-done.6
  54.6 6.8 %all_gather.33 = bf16[512,640]{1,0:T(8,128)(2,1)S(1)} all-gather(bf16[128,640]{1,0:T(8,128)(2,1)S(1)} %collective-permute-done.1), channel_id=1, replica_groups=mesh['rep'=4,'fsdp'=2,'seq'=4] {'seq'}, dimensions={0}, use_global_device_ids=true | all-gather | bytes 819200 | tf_op jit(solution)/shard_map/all_gather | solution.py:88
  63.2 5.7 %collective-permute-done.2 = bf16[80,4096]{1,0:T(8,128)(2,1)} collective-permute-done((bf16[80,4096]{1,0:T(8,128)(2,1)}, bf16[80,4096]{1,0:T(8,128)(2,1)}, u32[]{:S(2)}, u32[]{:S(2)}) %collective-permute-start.2) | collective-permute-done | bytes 655392 | tf_op jit(solution)/shard_map/ppermute | solution.py:68
  69.9 2.2 fusion.126
  74.0 1.6 copy.131
  75.6 2.3 reshape.502
  77.9 2.7 convolution_convert_fusion.6
  80.9 1.9 multiply_reduce_fusion.9
  83.2 3.4 broadcast_select_fusion.3
  86.7 10.9 %all-gather.11.cloned.1.call-done = bf16[320,4096]{1,0:T(8,128)(2,1)} async-done(((bf16[80,4096]{1,0:T(8,128)(2,1)}), bf16[320,4096]{1,0:T(8,128)(2,1)}) %all-gather.11.cloned.1.call-update) | async-done | bytes 2621456 | tf_op jit(solution)/shard_map/all_gather | solution.py:88
  97.6 2.9 broadcast_select_fusion.1
  100.5 1.9 fusion.5
  106.5 4.7 %fusion.23 = (bf16[256,2048]{1,0:T(8,128)(2,1)S(1)}, bf16[256,2048]{1,0:T(8,128)(2,1)S(1)}) fusion(f32[256,4096]{1,0:T(8,128)S(1)} %fusion.5, bf16[256,640]{1,0:T(8,128)(2,1)S(1)} %get-tuple-element.64, bf16[1024,640]{1,0:T(8,128)(2,1)S(1)} %copy-done.23, bf16[1024,640]{1,0:T(8,128)(2,1)S(1)} %copy-done.22), kind=kOutput, calls=%fused_computation.42 | convolution fusion | flops 688914432 | bytes 9240576 | tf_op jit(solution)/shard_map/dot_general | solution.py:51
  111.2 2.1 multiply_reduce_fusion.3
  113.3 1.7 convolution_convert_fusion
  115.0 2.1 constant_dynamic-slice_fusion.1
  117.1 1.8 copy.173
  123.0 1.9 convolution_convert_fusion.3
  130.0 2.8 fusion.71
  132.8 12.5 %fusion.38 = bf16[1024,256]{0,1:T(8,128)(2,1)} fusion(f32[256,4,1024]{2,0,1:T(8,128)} %fusion.71, f32[256,4,1024]{2,0,1:T(8,128)} %copy-done, f32[256,4]{0,1:T(4,128)S(1)} %log_add_fusion, bf16[256,4,128]{2,0,1:T(8,128)(2,1)} %copy-done.42, bf16[256,4,128]{2,0,1:T(8,128)(2,1)} %copy-done.41), kind=kOutput, calls=%fused_computation.73 | convolution fusion | flops 545523712 | bytes 9441280 | tf_op jit(solution)/shard_map/dot_general | solution.py:57
  145.3 2.6 convolution_convert_fusion.4
  147.9 3.0 fusion.1
  152.5 1.6 copy-done.4
  154.1 1.6 fusion.8
  159.5 2.3 copy.140
  161.8 12.3 %fusion.15 = f32[256,4,256]{2,0,1:T(8,128)} fusion(f32[256,4,1024]{2,0,1:T(8,128)} %fusion.71, f32[256,4,1024]{2,0,1:T(8,128)} %copy-done, f32[256,4]{0,1:T(4,128)S(1)} %log_add_fusion, bf16[1024,512]{1,0:T(8,128)(2,1)} %all-gather.9.cloned.1.call-done), kind=kOutput, calls=%fused_computation.33 | convolution fusion | flops 544212992 | bytes 18358272 | tf_op jit(solution)/shard_map/dot_general | solution.py:47
  174.1 1.5 multiply_add_fusion.1
  175.6 1.8 fusion.35
  177.4 5.9 %collective-permute-done.10 = bf16[2,80,4096]{2,1,0:T(8,128)(2,1)} collective-permute-done((bf16[2,80,4096]{2,1,0:T(8,128)(2,1)}, bf16[2,80,4096]{2,1,0:T(8,128)(2,1)}, u32[]{:S(2)}, u32[]{:S(2)}) %collective-permute-start.10) | collective-permute-done | bytes 1310752 | tf_op jit(solution)/shard_map/ppermute | solution.py:68
  183.4 1.7 fusion.9
  190.5 6.9 %collective-permute-done.14 = bf16[256,640]{1,0:T(8,128)(2,1)S(1)} collective-permute-done((bf16[256,640]{1,0:T(8,128)(2,1)S(1)}, bf16[256,640]{1,0:T(8,128)(2,1)S(1)}, u32[]{:S(2)}, u32[]{:S(2)}) %collective-permute-start.14) | collective-permute-done | bytes 327712 | tf_op jit(solution)/shard_map/ppermute | solution.py:68
  198.2 5.2 %collective-permute-done.11 = bf16[80,4096]{1,0:T(8,128)(2,1)} collective-permute-done((bf16[80,4096]{1,0:T(8,128)(2,1)}, bf16[80,4096]{1,0:T(8,128)(2,1)}, u32[]{:S(2)}, u32[]{:S(2)}) %collective-permute-start.11) | collective-permute-done | bytes 655392 | tf_op jit(solution)/shard_map/ppermute | solution.py:68
  203.4 2.3 fusion.36
  205.7 28.2 %all-reduce.10.cloned.1.call-done = bf16[256,640]{1,0:T(8,128)(2,1)} async-done(((bf16[256,640]{1,0:T(8,128)(2,1)}), bf16[256,640]{1,0:T(8,128)(2,1)}) %all-reduce.10.cloned.1.call-update) | async-done | bytes 327696 | tf_op jit(solution)/shard_map/psum | solution.py:105
  234.3 2.3 fusion.48
  236.6 2.0 copy.138
  240.0 1.5 collective-permute-start.5
  242.9 1.5 collective-permute-start.7
  244.5 2.0 collective-permute-done.5
  248.3 2.0 collective-permute-done.7
  253.0 2.8 collective-permute-done.8
  256.5 20.6 %all-reduce.12.cloned.1.call-done = bf16[80,4096]{1,0:T(8,128)(2,1)} async-done(((bf16[80,4096]{1,0:T(8,128)(2,1)}), bf16[80,4096]{1,0:T(8,128)(2,1)}) %all-reduce.12.cloned.1.call-update) | async-done | bytes 655376 | tf_op jit(solution)/shard_map/psum | solution.py:105
  278.2 18.0 %all-gather.15.cloned.1.call-done = bf16[1024,640]{1,0:T(8,128)(2,1)} async-done(((bf16[256,640]{1,0:T(8,128)(2,1)}), bf16[1024,640]{1,0:T(8,128)(2,1)}) %all-gather.15.cloned.1.call-update) | async-done | bytes 1310736 | tf_op jit(solution)/shard_map/all_gather | solution.py:106
  296.2 3.0 convert_element_type.437
  299.2 34.8 %all-reduce.14.cloned.1.call-done = bf16[128,640]{1,0:T(8,128)(2,1)} async-done(((bf16[128,640]{1,0:T(8,128)(2,1)}), bf16[128,640]{1,0:T(8,128)(2,1)}) %all-reduce.14.cloned.1.call-update) | async-done | bytes 163856 | tf_op jit(solution)/shard_map/psum | solution.py:105
  333.9 2.9 fusion.59
  336.8 2.0 convolution_convert_fusion.2
  339.4 2.8 collective-permute-done.15
  342.7 1.5 collective-permute-start.16
  344.2 13.9 %collective-permute-done.16 = bf16[2,96,1536]{2,1,0:T(8,128)(2,1)S(1)} collective-permute-done((bf16[2,96,1536]{2,1,0:T(8,128)(2,1)S(1)}, bf16[2,96,1536]{2,1,0:T(8,128)(2,1)S(1)}, u32[]{:S(2)}, u32[]{:S(2)}) %collective-permute-start.16) | collective-permute-done | bytes 589856 | tf_op jit(solution)/shard_map/ppermute | solution.py:68
  358.3 1.5 collective-permute-start.17
  359.8 6.8 %collective-permute-done.17 = bf16[96,1536]{1,0:T(8,128)(2,1)S(1)} collective-permute-done((bf16[96,1536]{1,0:T(8,128)(2,1)S(1)}, bf16[96,1536]{1,0:T(8,128)(2,1)S(1)}, u32[]{:S(2)}, u32[]{:S(2)}) %collective-permute-start.17) | collective-permute-done | bytes 294944 | tf_op jit(solution)/shard_map/ppermute | solution.py:68
  368.2 35.0 %all-reduce.16.cloned.1.call-done = bf16[96,1536]{1,0:T(8,128)(2,1)} async-done(((bf16[96,1536]{1,0:T(8,128)(2,1)}), bf16[96,1536]{1,0:T(8,128)(2,1)}) %all-reduce.16.cloned.1.call-update) | async-done | bytes 294928 | tf_op jit(solution)/shard_map/psum | solution.py:105
  403.2 7.9 %all_gather.38 = bf16[512,640]{1,0:T(8,128)(2,1)S(1)} all-gather(bf16[128,640]{1,0:T(8,128)(2,1)S(1)} %copy-done.44), channel_id=1, replica_groups=mesh['rep'=4,'fsdp'=2,'seq'=4] {'seq'}, dimensions={0}, use_global_device_ids=true | all-gather | bytes 819200 | tf_op jit(solution)/shard_map/all_gather | solution.py:106
  413.2 16.9 %all-gather.19.cloned.1.call-done = bf16[320,4096]{1,0:T(8,128)(2,1)} async-done(((bf16[80,4096]{1,0:T(8,128)(2,1)}), bf16[320,4096]{1,0:T(8,128)(2,1)}) %all-gather.19.cloned.1.call-update) | async-done | bytes 2621456 | tf_op jit(solution)/shard_map/all_gather | solution.py:106
  430.0 4.8 %fusion.124 = (f32[320,2048]{1,0:T(8,128)}, f32[320,2048]{1,0:T(8,128)}) fusion(bf16[320,4096]{1,0:T(8,128)(2,1)} %all-gather.19.cloned.1.call-done), kind=kLoop, calls=%fused_computation.269 | loop fusion | bytes 10485760 | tf_op jit(solution)/shard_map/slice | solution.py:314
  434.8 14.1 %all-gather.17.cloned.1.call-done = bf16[384,1536]{1,0:T(8,128)(2,1)} async-done(((bf16[96,1536]{1,0:T(8,128)(2,1)}), bf16[384,1536]{1,0:T(8,128)(2,1)}) %all-gather.17.cloned.1.call-update) | async-done | bytes 1179664 | tf_op jit(solution)/shard_map/all_gather | solution.py:106
  (257 shorter events, 63.7 us)
Async XLA Ops:
  7.2 6.3 %copy-start.51 = (s32[1,3]{1,0:T(1,128)S(1)}, s32[1,3]{1,0:T(1,128)}, u32[]{:S(2)}) copy-start(s32[1,3]{1,0:T(1,128)} %param.18) | copy-start | bytes 40
  7.2 6.5 %copy-start.9 = (bf16[1,256,640]{2,1,0:T(8,128)(2,1)S(1)}, bf16[1,256,640]{2,1,0:T(8,128)(2,1)}, u32[]{:S(2)}) copy-start(bf16[1,256,640]{2,1,0:T(8,128)(2,1)} %param.16) | copy-start | bytes 983044
  7.2 6.8 %copy-start.48 = (bf16[320]{0:T(512)(128)(2,1)S(1)}, bf16[320]{0:T(512)(128)(2,1)}, u32[]{:S(2)}) copy-start(bf16[320]{0:T(512)(128)(2,1)} %param.31) | copy-start | bytes 1924
  7.2 6.8 %copy-start.47 = (bf16[320]{0:T(512)(128)(2,1)S(1)}, bf16[320]{0:T(512)(128)(2,1)}, u32[]{:S(2)}) copy-start(bf16[320]{0:T(512)(128)(2,1)} %param.30) | copy-start | bytes 1924
  7.2 6.8 %copy-start.46 = (bf16[320]{0:T(512)(128)(2,1)S(1)}, bf16[320]{0:T(512)(128)(2,1)}, u32[]{:S(2)}) copy-start(bf16[320]{0:T(512)(128)(2,1)} %param.29) | copy-start | bytes 1924
  7.2 6.8 %copy-start.50 = (bf16[128]{0:T(256)(128)(2,1)S(1)}, bf16[128]{0:T(256)(128)(2,1)}, u32[]{:S(2)}) copy-start(bf16[128]{0:T(256)(128)(2,1)} %param.28) | copy-start | bytes 772
  7.2 6.8 %copy-start.49 = (bf16[128]{0:T(256)(128)(2,1)S(1)}, bf16[128]{0:T(256)(128)(2,1)}, u32[]{:S(2)}) copy-start(bf16[128]{0:T(256)(128)(2,1)} %param.27) | copy-start | bytes 772
  7.3 6.8 %copy-start.45 = (bf16[320]{0:T(512)(128)(2,1)S(1)}, bf16[320]{0:T(512)(128)(2,1)}, u32[]{:S(2)}) copy-start(bf16[320]{0:T(512)(128)(2,1)} %param.26) | copy-start | bytes 1924
  7.3 62.6 %all-gather.9.cloned.1.call-start = ((), (), s32[]{:S(2)}) async-start(), calls=%async_computation | async-start | bytes 1310720 | tf_op jit(solution)/shard_map/all_gather | solution.py:206
  10.4 9.5 %collective-permute-start = (bf16[80,1536]{1,0:T(8,128)(2,1)S(1)}, bf16[80,1536]{1,0:T(8,128)(2,1)S(1)}, u32[]{:S(2)}, u32[]{:S(2)}) collective-permute-start(bf16[80,1536]{1,0:T(8,128)(2,1)S(1)} %constant_dynamic-slice_fusion.5), channel_id=1, source_target_pairs={{0,4},{4,0},{1,5},{5,1},{2,6},{6,2},{3,7},{7,3},{8,12},{12,8},{9,1... | collective-permute-start | bytes 737288 | tf_op jit(solution)/shard_map/ppermute | solution.py:68
  31.3 31.3 %copy-start.15 = (f32[256,1536]{1,0:T(8,128)}, f32[256,1536]{1,0:T(8,128)S(1)}, u32[]{:S(2)}) copy-start(f32[256,1536]{1,0:T(8,128)S(1)} %fusion.42) | copy-start | bytes 4718596
  31.3 14.4 %copy-start.30 = (bf16[512,640]{1,0:T(8,128)(2,1)S(1)}, bf16[512,640]{1,0:T(8,128)(2,1)}, u32[]{:S(2)}) copy-start(bf16[512,640]{1,0:T(8,128)(2,1)} %param.22) | copy-start | bytes 1966084
  32.2 37.5 %copy-start.27 = (f32[256,128]{1,0:T(8,128)}, f32[256,128]{1,0:T(8,128)S(1)}, u32[]{:S(2)}) copy-start(f32[256,128]{1,0:T(8,128)S(1)} %get-tuple-element.78) | copy-start | bytes 393220
  32.2 37.5 %copy-start.29 = (f32[256,128]{1,0:T(8,128)}, f32[256,128]{1,0:T(8,128)S(1)}, u32[]{:S(2)}) copy-start(f32[256,128]{1,0:T(8,128)S(1)} %get-tuple-element.79) | copy-start | bytes 393220
  33.0 50.2 %all-gather.13.cloned.1.call-start = ((), (), s32[]{:S(2)}) async-start(), calls=%async_computation.2 | async-start | bytes 1638400 | tf_op jit(solution)/shard_map/all_gather | solution.py:88
  34.8 10.2 %collective-permute-start.3 = (bf16[256,640]{1,0:T(8,128)(2,1)}, bf16[256,640]{1,0:T(8,128)(2,1)S(1)}, u32[]{:S(2)}, u32[]{:S(2)}) collective-permute-start(bf16[256,640]{1,0:T(8,128)(2,1)} %constant_dynamic-slice_fusion.2), channel_id=1, source_target_pairs={{0,4},{4,0},{1,5},{5,1},{2,6},{6,2},{3,7},{7,3},{8,12},{12,8},{9,1... | collective-permute-start | bytes 983048 | tf_op jit(solution)/shard_map/ppermute | solution.py:68
  45.7 51.9 %all-gather.11.cloned.1.call-start = ((), (), s32[]{:S(2)}) async-start(), calls=%async_computation.1 | async-start | bytes 3276800 | tf_op jit(solution)/shard_map/all_gather | solution.py:88
  45.8 8.8 %collective-permute-start.1 = (bf16[128,640]{1,0:T(8,128)(2,1)S(1)}, bf16[128,640]{1,0:T(8,128)(2,1)S(1)}, u32[]{:S(2)}, u32[]{:S(2)}) collective-permute-start(bf16[128,640]{1,0:T(8,128)(2,1)S(1)} %constant_dynamic-slice_fusion.4), channel_id=1, source_target_pairs={{0,4},{4,0},{1,5},{5,1},{2,6},{6,2},{3,7},{7,3},{8,12},{12,8},{9,1... | collective-permute-start | bytes 491528 | tf_op jit(solution)/shard_map/ppermute | solution.py:68
  52.7 16.3 %collective-permute-start.2 = (bf16[80,4096]{1,0:T(8,128)(2,1)}, bf16[80,4096]{1,0:T(8,128)(2,1)}, u32[]{:S(2)}, u32[]{:S(2)}) collective-permute-start(bf16[80,4096]{1,0:T(8,128)(2,1)} %constant_dynamic-slice_fusion.3), channel_id=1, source_target_pairs={{0,4},{4,0},{1,5},{5,1},{2,6},{6,2},{3,7},{7,3},{8,12},{12,8},{9,1... | collective-permute-start | bytes 1966088 | tf_op jit(solution)/shard_map/ppermute | solution.py:68
  69.0 165.0 %all-reduce.10.cloned.1.call-start = ((), (), s32[]{:S(2)}) async-start(), calls=%async_computation.3 | async-start | bytes 655360 | tf_op jit(solution)/shard_map/psum | solution.py:105
  69.8 2.2 copy-start.41
  69.8 2.2 copy-start.42
  77.9 3.0 copy-start.35
  80.9 2.0 copy-start.21
  103.1 2.1 copy-start.13
  106.5 4.7 %copy-start.25 = (bf16[256,640]{1,0:T(8,128)(2,1)}, bf16[256,640]{1,0:T(8,128)(2,1)S(1)}, u32[]{:S(2)}) copy-start(bf16[256,640]{1,0:T(8,128)(2,1)S(1)} %get-tuple-element.64) | copy-start | bytes 983044
  118.9 29.0 %collective-permute-start.9 = (bf16[2,2,80,4096]{3,2,0,1:T(8,128)(2,1)}, bf16[2,2,80,4096]{3,2,0,1:T(8,128)(2,1)}, u32[]{:S(2)}, u32[]{:S(2)}) collective-permute-start(bf16[2,2,80,4096]{3,2,0,1:T(8,128)(2,1)} %bitcast.188), channel_id=1, source_target_pairs={{0,1},{1,0},{2,3},{3,2},{4,5},{5,4},{6,7},{7,6},{8,9},{9,8},{10,11... | collective-permute-start | bytes 7864328 | tf_op jit(solution)/shard_map/ppermute | solution.py:68
  123.0 3.1 copy-start.14
  123.0 3.1 copy-start.26
  125.8 4.2 copy-start.20
  125.8 4.2 copy-start.40
  125.8 115.8 %collective-permute-start.6 = (bf16[2,2,128,640]{3,2,1,0:T(8,128)(2,1)}, bf16[2,2,128,640]{3,2,1,0:T(8,128)(2,1)}, u32[]{:S(2)}, u32[]{:S(2)}) collective-permute-start(bf16[2,2,128,640]{3,2,1,0:T(8,128)(2,1)} %dynamic-slice_bitcast_fusion.4), channel_id=1, source_target_pairs={{0,1},{1,0},{2,3},{3,2},{4,5},{5,4},{6,7},{7,6},{8,9},{9,8},{10,11... | collective-permute-start | bytes 1966088 | tf_op jit(solution)/shard_map/ppermute | solution.py:68
  129.8 22.7 %collective-permute-start.12 = (bf16[2,2,256,640]{3,2,1,0:T(8,128)(2,1)}, bf16[2,2,256,640]{3,2,1,0:T(8,128)(2,1)}, u32[]{:S(2)}, u32[]{:S(2)}) collective-permute-start(bf16[2,2,256,640]{3,2,1,0:T(8,128)(2,1)} %dynamic-slice_bitcast_fusion), channel_id=1, source_target_pairs={{0,1},{1,0},{2,3},{3,2},{4,5},{5,4},{6,7},{7,6},{8,9},{9,8},{10,11... | collective-permute-start | bytes 3932168 | tf_op jit(solution)/shard_map/ppermute | solution.py:68
  145.3 2.6 copy-start.5
  150.9 4.8 %copy-start.1 = (bf16[2,2,80,4096]{3,2,0,1:T(8,128)(2,1)}, bf16[2,2,80,4096]{3,2,0,1:T(8,128)(2,1)S(1)}, u32[]{:S(2)}) copy-start(bf16[2,2,80,4096]{3,2,0,1:T(8,128)(2,1)S(1)} %fusion.1) | copy-start | bytes 7864324
  150.9 3.2 copy-start.4
  152.1 6.4 %copy-start.38 = (bf16[1024,256]{0,1:T(8,128)(2,1)S(1)}, bf16[1024,256]{0,1:T(8,128)(2,1)}, u32[]{:S(2)}) copy-start(bf16[1024,256]{0,1:T(8,128)(2,1)} %fusion.38) | copy-start | bytes 1572868
  152.1 31.3 %collective-permute-start.10 = (bf16[2,80,4096]{2,1,0:T(8,128)(2,1)}, bf16[2,80,4096]{2,1,0:T(8,128)(2,1)}, u32[]{:S(2)}, u32[]{:S(2)}) collective-permute-start(bf16[2,80,4096]{2,1,0:T(8,128)(2,1)} %dynamic-slice_bitcast_fusion.1), channel_id=1, source_target_pairs={{0,2},{1,3},{2,0},{3,1},{4,6},{5,7},{6,4},{7,5},{8,10},{9,11},{10,... | collective-permute-start | bytes 3932168 | tf_op jit(solution)/shard_map/ppermute | solution.py:68
  157.0 18.6 %collective-permute-start.13 = (bf16[2,256,640]{2,1,0:T(8,128)(2,1)}, bf16[2,256,640]{2,1,0:T(8,128)(2,1)}, u32[]{:S(2)}, u32[]{:S(2)}) collective-permute-start(bf16[2,256,640]{2,1,0:T(8,128)(2,1)} %dynamic-slice_bitcast_fusion.2), channel_id=1, source_target_pairs={{0,4},{4,0},{1,5},{5,1},{2,6},{6,2},{3,7},{7,3},{8,12},{12,8},{9,1... | collective-permute-start | bytes 1966088 | tf_op jit(solution)/shard_map/ppermute | solution.py:68
  161.8 12.3 %copy-start.28 = (f32[256,128]{1,0:T(8,128)S(1)}, f32[256,128]{1,0:T(8,128)}, u32[]{:S(2)}) copy-start(f32[256,128]{1,0:T(8,128)} %copy-done.27) | copy-start | bytes 393220
  174.1 9.3 %copy-start.2 = (bf16[2,2,80,4096]{3,2,0,1:T(8,128)(2,1)S(1)}, bf16[2,2,80,4096]{3,2,0,1:T(8,128)(2,1)}, u32[]{:S(2)}) copy-start(bf16[2,2,80,4096]{3,2,0,1:T(8,128)(2,1)} %copy-done.1) | copy-start | bytes 7864324
  175.6 14.4 %copy-start.10 = (f32[256,4,128]{2,0,1:T(8,128)}, f32[256,4,128]{2,0,1:T(8,128)S(1)}, u32[]{:S(2)}) copy-start(f32[256,4,128]{2,0,1:T(8,128)S(1)} %get-tuple-element.58) | copy-start | bytes 1572868
  175.6 14.4 %copy-start.11 = (f32[256,4,128]{2,0,1:T(8,128)}, f32[256,4,128]{2,0,1:T(8,128)S(1)}, u32[]{:S(2)}) copy-start(f32[256,4,128]{2,0,1:T(8,128)S(1)} %get-tuple-element.59) | copy-start | bytes 1572868
  177.4 11.7 %copy-start.12 = (bf16[1024,512]{1,0:T(8,128)(2,1)S(1)}, bf16[1024,512]{1,0:T(8,128)(2,1)}, u32[]{:S(2)}) copy-start(bf16[1024,512]{1,0:T(8,128)(2,1)} %copy.140) | copy-start | bytes 3145732
  187.1 16.4 %collective-permute-start.11 = (bf16[80,4096]{1,0:T(8,128)(2,1)}, bf16[80,4096]{1,0:T(8,128)(2,1)}, u32[]{:S(2)}, u32[]{:S(2)}) collective-permute-start(bf16[80,4096]{1,0:T(8,128)(2,1)} %dynamic-slice_bitcast_fusion.3), channel_id=1, source_target_pairs={{0,4},{4,0},{1,5},{5,1},{2,6},{6,2},{3,7},{7,3},{8,12},{12,8},{9,1... | collective-permute-start | bytes 1966088 | tf_op jit(solution)/shard_map/ppermute | solution.py:68
  188.5 8.8 %collective-permute-start.14 = (bf16[256,640]{1,0:T(8,128)(2,1)S(1)}, bf16[256,640]{1,0:T(8,128)(2,1)S(1)}, u32[]{:S(2)}, u32[]{:S(2)}) collective-permute-start(bf16[256,640]{1,0:T(8,128)(2,1)S(1)} %dynamic-slice_bitcast_fusion.7), channel_id=1, source_target_pairs={{0,2},{1,3},{2,0},{3,1},{4,6},{5,7},{6,4},{7,5},{8,10},{9,11},{10,... | collective-permute-start | bytes 983048 | tf_op jit(solution)/shard_map/ppermute | solution.py:68
  190.0 48.6 %collective-permute-start.4 = (bf16[2,256,512]{2,1,0:T(8,128)(2,1)}, bf16[2,256,512]{2,1,0:T(8,128)(2,1)}, u32[]{:S(2)}, u32[]{:S(2)}) collective-permute-start(bf16[2,256,512]{2,1,0:T(8,128)(2,1)} %dynamic-slice_bitcast_fusion.6), channel_id=1, source_target_pairs={{0,1},{1,0},{2,3},{3,2},{4,5},{5,4},{6,7},{7,6},{8,9},{9,8},{10,11... | collective-permute-start | bytes 1572872 | tf_op jit(solution)/shard_map/ppermute | solution.py:68
  198.2 78.9 %all-reduce.12.cloned.1.call-start = ((), (), s32[]{:S(2)}) async-start(), calls=%async_computation.4 | async-start | bytes 1310720 | tf_op jit(solution)/shard_map/psum | solution.py:105
  233.9 62.3 %all-gather.15.cloned.1.call-start = ((), (), s32[]{:S(2)}) async-start(), calls=%async_computation.6 | async-start | bytes 1638400 | tf_op jit(solution)/shard_map/all_gather | solution.py:106
  240.0 6.4 %collective-permute-start.5 = (bf16[256,512]{1,0:T(8,128)(2,1)S(1)}, bf16[256,512]{1,0:T(8,128)(2,1)S(1)}, u32[]{:S(2)}, u32[]{:S(2)}) collective-permute-start(bf16[256,512]{1,0:T(8,128)(2,1)S(1)} %dynamic-slice_bitcast_fusion.10), channel_id=1, source_target_pairs={{0,2},{1,3},{2,0},{3,1},{4,6},{5,7},{6,4},{7,5},{8,10},{9,11},{10,... | collective-permute-start | bytes 786440 | tf_op jit(solution)/shard_map/ppermute | solution.py:68
  241.6 92.4 %all-reduce.14.cloned.1.call-start = ((), (), s32[]{:S(2)}) async-start(), calls=%async_computation.5 | async-start | bytes 327680 | tf_op jit(solution)/shard_map/psum | solution.py:105
  242.9 7.3 %collective-permute-start.7 = (bf16[2,128,640]{2,1,0:T(8,128)(2,1)S(1)}, bf16[2,128,640]{2,1,0:T(8,128)(2,1)S(1)}, u32[]{:S(2)}, u32[]{:S(2)}) collective-permute-start(bf16[2,128,640]{2,1,0:T(8,128)(2,1)S(1)} %dynamic-slice_bitcast_fusion.8), channel_id=1, source_target_pairs={{0,4},{4,0},{1,5},{5,1},{2,6},{6,2},{3,7},{7,3},{8,12},{12,8},{9,1... | collective-permute-start | bytes 983048 | tf_op jit(solution)/shard_map/ppermute | solution.py:68
  246.6 30.6 %copy-start.18 = (bf16[256,4,256]{0,2,1:T(8,128)(2,1)S(1)}, bf16[256,4,256]{0,2,1:T(8,128)(2,1)}, u32[]{:S(2)}) copy-start(bf16[256,4,256]{0,2,1:T(8,128)(2,1)} %copy.138) | copy-start | bytes 1572868
  250.4 5.4 %collective-permute-start.8 = (bf16[128,640]{1,0:T(8,128)(2,1)S(1)}, bf16[128,640]{1,0:T(8,128)(2,1)S(1)}, u32[]{:S(2)}, u32[]{:S(2)}) collective-permute-start(bf16[128,640]{1,0:T(8,128)(2,1)S(1)} %dynamic-slice_bitcast_fusion.11), channel_id=1, source_target_pairs={{0,2},{1,3},{2,0},{3,1},{4,6},{5,7},{6,4},{7,5},{8,10},{9,11},{10,... | collective-permute-start | bytes 491528 | tf_op jit(solution)/shard_map/ppermute | solution.py:68
  277.1 126.1 %all-reduce.16.cloned.1.call-start = ((), (), s32[]{:S(2)}) async-start(), calls=%async_computation.7 | async-start | bytes 589824 | tf_op jit(solution)/shard_map/psum | solution.py:105
  277.1 56.8 %copy-start.32 = (bf16[320,1536]{1,0:T(8,128)(2,1)S(1)}, bf16[320,1536]{1,0:T(8,128)(2,1)}, u32[]{:S(2)}) copy-start(bf16[320,1536]{1,0:T(8,128)(2,1)} %copy-done.31) | copy-start | bytes 2949124
  278.2 55.8 %copy-start.16 = (bf16[256,1536]{0,1:T(8,128)(2,1)}, bf16[256,1536]{0,1:T(8,128)(2,1)S(1)}, u32[]{:S(2)}) copy-start(bf16[256,1536]{0,1:T(8,128)(2,1)S(1)} %pad_maximum_fusion.16) | copy-start | bytes 2359300
  339.4 2.9 collective-permute-start.15
  342.7 60.5 %copy-start.44 = (bf16[128,640]{1,0:T(8,128)(2,1)S(1)}, bf16[128,640]{1,0:T(8,128)(2,1)}, u32[]{:S(2)}) copy-start(bf16[128,640]{1,0:T(8,128)(2,1)} %all-reduce.14.cloned.1.call-done) | copy-start | bytes 491524
  342.7 15.4 %collective-permute-start.16 = (bf16[2,96,1536]{2,1,0:T(8,128)(2,1)S(1)}, bf16[2,96,1536]{2,1,0:T(8,128)(2,1)S(1)}, u32[]{:S(2)}, u32[]{:S(2)}) collective-permute-start(bf16[2,96,1536]{2,1,0:T(8,128)(2,1)S(1)} %dynamic-slice_bitcast_fusion.5), channel_id=1, source_target_pairs={{0,4},{4,0},{1,5},{5,1},{2,6},{6,2},{3,7},{7,3},{8,12},{12,8},{9,1... | collective-permute-start | bytes 1769480 | tf_op jit(solution)/shard_map/ppermute | solution.py:68
  358.3 53.9 %copy-start.34 = (f32[256,640]{1,0:T(8,128)S(1)}, f32[256,640]{1,0:T(8,128)}, u32[]{:S(2)}) copy-start(f32[256,640]{1,0:T(8,128)} %get-tuple-element.89) | copy-start | bytes 1966084
  358.3 8.3 %collective-permute-start.17 = (bf16[96,1536]{1,0:T(8,128)(2,1)S(1)}, bf16[96,1536]{1,0:T(8,128)(2,1)S(1)}, u32[]{:S(2)}, u32[]{:S(2)}) collective-permute-start(bf16[96,1536]{1,0:T(8,128)(2,1)S(1)} %dynamic-slice_bitcast_fusion.9), channel_id=1, source_target_pairs={{0,2},{1,3},{2,0},{3,1},{4,6},{5,7},{6,4},{7,5},{8,10},{9,11},{10,... | collective-permute-start | bytes 884744 | tf_op jit(solution)/shard_map/ppermute | solution.py:68
  367.4 62.7 %all-gather.19.cloned.1.call-start = ((), (), s32[]{:S(2)}) async-start(), calls=%async_computation.9 | async-start | bytes 3276800 | tf_op jit(solution)/shard_map/all_gather | solution.py:106
  368.1 80.8 %all-gather.17.cloned.1.call-start = ((), (), s32[]{:S(2)}) async-start(), calls=%async_computation.8 | async-start | bytes 1474560 | tf_op jit(solution)/shard_map/all_gather | solution.py:106
  (16 other events, 20.1 us)
Sparse Core Ops, SparseCore 0:
  33.1 16.9 all-gather.8
  52.3 18.1 all-gather.12
  72.0 25.5 all-gather.10
  198.3 35.5 all-reduce.9
  236.7 40.3 all-reduce.11
  278.5 17.6 all-gather.14
  299.1 34.8 all-reduce.13
  367.5 35.5 all-reduce.15
  404.7 25.2 all-gather.18
  431.5 17.4 all-gather.16
